TPU v7x, 256 devices: a whole 4x4x8 slice. The times are simulated.
256 devices in a mesh: row: 16 (over z, core), col: 16 (over x, y).
Axes of the slice: x: 4, y: 4, z: 8, core: 2. Of those that a mesh axis runs over, the one named last changes fastest.
Arguments:
- gen_showers: bfloat16 [16384, 6480], P(('row', 'col')), may hold values from -10 to 10
- ref_showers: bfloat16 [16384, 6480], P(('row', 'col')), may hold values from -10 to 10
- w_in: bfloat16 [6480, 512], replicated, may hold values from -0.078125 to 0.078125
- b_in: float32 [512], replicated, may hold values from -4 to 4
- w_out: bfloat16 [512, 256], replicated, may hold values from -0.25 to 0.25
Outputs:
- gen_potential: float32 [16384], P('row')
- ref_potential: float32 [16, 1024], P(None, 'col')
All inputs are finite; a program needn't handle non-finite values.
Results may differ from a plain program's by a relative error of at most 0.0003.
Values sent between devices are 32-bit elements; how exact they have to be, the bound alone decides.
A program may use at most 128 MiB of HBM per device.

v0:
```python
import math
import jax
import jax.numpy as jnp
from jax import lax
from jax.sharding import PartitionSpec as P

ITERS = 3
EPSILON = 0.1


def embed(showers, w_in, b_in, w_out):
    hidden = jnp.dot(showers, w_in, preferred_element_type=jnp.float32) + b_in
    hidden = jnp.maximum(hidden, 0.0)
    features = jnp.dot(hidden, w_out.astype(jnp.float32), precision=lax.Precision.HIGHEST)
    squares = jnp.sum(jnp.square(features), axis=1)
    return (features, squares)


def reduce_cols(scaled):
    largest = lax.pmax(jnp.max(scaled, axis=1), "col")
    totals = lax.psum(jnp.sum(jnp.exp(scaled - largest[:, None]), axis=1), "col")
    return -EPSILON * (largest + jnp.log(totals))


def reduce_rows(scaled):
    largest = lax.pmax(jnp.max(scaled, axis=0), "row")
    totals = lax.psum(jnp.sum(jnp.exp(scaled - largest[None, :]), axis=0), "row")
    return -EPSILON * (largest + jnp.log(totals))


def body(gen_showers, ref_showers, w_in, b_in, w_out):
    gen_feat, gen_sq = embed(gen_showers, w_in, b_in, w_out)
    ref_feat, ref_sq = embed(ref_showers, w_in, b_in, w_out)
    row_count = lax.axis_size("row")
    col_count = lax.axis_size("col")
    per_dev = gen_feat.shape[0]
    width = gen_feat.shape[1]
    gen_rows, gen_norms = (
        lax.all_gather(gen_feat, "col", axis=0, tiled=True),
        lax.all_gather(gen_sq, "col", axis=0, tiled=True),
    )
    ref_cols, ref_norms = (
        lax.all_gather(ref_feat, "row", axis=0, tiled=True),
        lax.all_gather(ref_sq, "row", axis=0, tiled=True),
    )
    total_count = row_count * col_count * per_dev
    log_weight = -math.log(total_count)

    def tile_cost():
        inner_prod = lax.dot_general(
            gen_rows,
            ref_cols,
            (((1,), (1,)), ((), ())),
            precision=lax.Precision.HIGHEST,
            preferred_element_type=jnp.float32,
        )
        return (gen_norms[:, None] + ref_norms[None, :] - 2.0 * inner_prod) / width

    ref_pot = jnp.zeros((ref_cols.shape[0],), jnp.float32)
    gen_pot = jnp.zeros((gen_rows.shape[0],), jnp.float32)
    for sweep_idx in range(ITERS):
        scaled = log_weight + (ref_pot[None, :] - tile_cost()) / EPSILON
        gen_pot = reduce_cols(scaled)
        scaled = log_weight + (gen_pot[:, None] - tile_cost()) / EPSILON
        ref_pot = reduce_rows(scaled)
    return (gen_pot, ref_pot.reshape(row_count, per_dev))


def solution(mesh):
    return jax.shard_map(
        body,
        mesh=mesh,
        in_specs=(P(("row", "col"), None), P(("row", "col"), None), P(), P(), P()),
        out_specs=(P("row"), P(None, "col")),
        check_vma=False,
    )
```

profile of v0, /device:TPU:1, one launch (start us, length us, event | category | flops | bytes accessed | tf_op | source)
XLA Modules:
  0.0 517.0 jit_solution(4666240185190480455)
XLA Ops:
  7.3 1.1 copy-done
  8.4 4.1 fusion.7
  12.6 1.0 multiply_reduce_fusion.1
  13.7 4.1 fusion.6
  17.8 1.0 multiply_reduce_fusion
  21.8 34.3 %all-reduce = f32[1024]{0:T(1024)S(1)} all-reduce(f32[1024]{0:T(1024)S(1)} %dynamic-update-slice), channel_id=1, replica_groups=mesh['row'=16,'col'=16] {'col'}, use_global_device_ids=true, to_apply=%add | all-reduce | flops 1024 | bytes 8192
  56.1 34.0 %all-reduce.1 = f32[1024]{0:T(1024)S(1)} all-reduce(f32[1024]{0:T(1024)S(1)} %dynamic-update-slice.1), channel_id=1, replica_groups=mesh['row'=16,'col'=16] {'row'}, use_global_device_ids=true, to_apply=%add.1 | all-reduce | flops 1024 | bytes 8192
  90.2 14.9 %all-gather.5.cloned.1.call-done = f32[1024,256]{1,0:T(8,128)} async-done(((f32[64,256]{1,0:T(8,128)}), f32[1024,256]{1,0:T(8,128)}) %all-gather.5.cloned.1.call-update) | async-done | bytes 1048592 | tf_op jit(solution)/shard_map/all_gather | solution.py:43
  105.1 7.9 %fusion = (f32[1024]{0:T(1024)S(1)}, f32[1024,1024]{1,0:T(8,128)}) fusion(f32[1024,256]{1,0:T(8,128)} %all-gather.3.cloned.1.call-done, f32[1024,256]{1,0:T(8,128)} %all-gather.5.cloned.1.call-done, f32[1024]{0:T(1024)S(1)} %all-reduce.1, f32[1024]{0:T(1024)S(1)} %all-reduce), kind=kOutput, calls=%fused_computation.13 | convolution fusion | flops 3229613056 | bytes 6303744 | tf_op jit(solution)/shard_map/dot_general | solution.py:50
  113.0 33.2 %pmax.42 = f32[1024]{0:T(1024)S(1)} all-reduce(f32[1024]{0:T(1024)S(1)} %get-tuple-element.6), channel_id=1, replica_groups=mesh['row'=16,'col'=16] {'col'}, use_global_device_ids=true, to_apply=%region_3.0 | all-reduce | flops 1024 | bytes 8192 | tf_op jit(solution)/shard_map/pmax | solution.py:20
  146.2 3.3 exponential_reduce_fusion.5
  149.5 28.5 %psum.42 = f32[1024]{0:T(1024)S(1)} all-reduce(f32[1024]{0:T(1024)S(1)} %exponential_reduce_fusion.5), channel_id=1, replica_groups=mesh['row'=16,'col'=16] {'col'}, use_global_device_ids=true, to_apply=%region_5.0 | all-reduce | flops 1024 | bytes 8192 | tf_op jit(solution)/shard_map/psum | solution.py:21
  178.0 2.8 fusion.1
  180.8 37.2 %pmax.43 = f32[1024]{0:T(1024)S(1)} all-reduce(f32[1024]{0:T(1024)S(1)} %fusion.1), channel_id=1, replica_groups=mesh['row'=16,'col'=16] {'row'}, use_global_device_ids=true, to_apply=%region_7.0 | all-reduce | flops 1024 | bytes 8192 | tf_op jit(solution)/shard_map/pmax | solution.py:26
  218.1 3.2 exponential_reduce_fusion.4
  221.3 23.6 %psum.43 = f32[1024]{0:T(1024)S(1)} all-reduce(f32[1024]{0:T(1024)S(1)} %exponential_reduce_fusion.4), channel_id=1, replica_groups=mesh['row'=16,'col'=16] {'row'}, use_global_device_ids=true, to_apply=%region_9.0 | all-reduce | flops 1024 | bytes 8192 | tf_op jit(solution)/shard_map/psum | solution.py:27
  244.8 2.8 fusion.2
  247.7 30.4 %pmax.44 = f32[1024]{0:T(1024)S(1)} all-reduce(f32[1024]{0:T(1024)S(1)} %fusion.2), channel_id=1, replica_groups=mesh['row'=16,'col'=16] {'col'}, use_global_device_ids=true, to_apply=%region_11.0 | all-reduce | flops 1024 | bytes 8192 | tf_op jit(solution)/shard_map/pmax | solution.py:20
  278.1 3.3 exponential_reduce_fusion.3
  281.4 28.5 %psum.44 = f32[1024]{0:T(1024)S(1)} all-reduce(f32[1024]{0:T(1024)S(1)} %exponential_reduce_fusion.3), channel_id=1, replica_groups=mesh['row'=16,'col'=16] {'col'}, use_global_device_ids=true, to_apply=%region_13.0 | all-reduce | flops 1024 | bytes 8192 | tf_op jit(solution)/shard_map/psum | solution.py:21
  309.9 2.8 fusion.3
  312.7 37.7 %pmax.45 = f32[1024]{0:T(1024)S(1)} all-reduce(f32[1024]{0:T(1024)S(1)} %fusion.3), channel_id=1, replica_groups=mesh['row'=16,'col'=16] {'row'}, use_global_device_ids=true, to_apply=%region_15.0 | all-reduce | flops 1024 | bytes 8192 | tf_op jit(solution)/shard_map/pmax | solution.py:26
  350.4 3.2 exponential_reduce_fusion.2
  353.7 23.6 %psum.45 = f32[1024]{0:T(1024)S(1)} all-reduce(f32[1024]{0:T(1024)S(1)} %exponential_reduce_fusion.2), channel_id=1, replica_groups=mesh['row'=16,'col'=16] {'row'}, use_global_device_ids=true, to_apply=%region_17.0 | all-reduce | flops 1024 | bytes 8192 | tf_op jit(solution)/shard_map/psum | solution.py:27
  377.2 2.8 fusion.4
  380.0 30.2 %pmax.46 = f32[1024]{0:T(1024)S(1)} all-reduce(f32[1024]{0:T(1024)S(1)} %fusion.4), channel_id=1, replica_groups=mesh['row'=16,'col'=16] {'col'}, use_global_device_ids=true, to_apply=%region_19.0 | all-reduce | flops 1024 | bytes 8192 | tf_op jit(solution)/shard_map/pmax | solution.py:20
  410.3 3.3 exponential_reduce_fusion.1
  413.6 28.5 %psum.46 = f32[1024]{0:T(1024)S(1)} all-reduce(f32[1024]{0:T(1024)S(1)} %exponential_reduce_fusion.1), channel_id=1, replica_groups=mesh['row'=16,'col'=16] {'col'}, use_global_device_ids=true, to_apply=%region_21.0 | all-reduce | flops 1024 | bytes 8192 | tf_op jit(solution)/shard_map/psum | solution.py:21
  442.1 2.8 fusion.5
  444.9 37.8 %pmax.47 = f32[1024]{0:T(1024)S(1)} all-reduce(f32[1024]{0:T(1024)S(1)} %fusion.5), channel_id=1, replica_groups=mesh['row'=16,'col'=16] {'row'}, use_global_device_ids=true, to_apply=%region_23.0 | all-reduce | flops 1024 | bytes 8192 | tf_op jit(solution)/shard_map/pmax | solution.py:26
  482.7 3.2 exponential_reduce_fusion
  485.9 23.6 %psum.47 = f32[1024]{0:T(1024)S(1)} all-reduce(f32[1024]{0:T(1024)S(1)} %exponential_reduce_fusion), channel_id=1, replica_groups=mesh['row'=16,'col'=16] {'row'}, use_global_device_ids=true, to_apply=%region_25.0 | all-reduce | flops 1024 | bytes 8192 | tf_op jit(solution)/shard_map/psum | solution.py:27
  (31 shorter events, 2.5 us)
Async XLA Ops:
  7.2 1.2 copy-start
  7.2 6.5 %copy-start.4 = (f32[512]{0:T(512)S(1)}, f32[512]{0:T(512)}, u32[]{:S(2)}) copy-start(f32[512]{0:T(512)} %param.8) | copy-start | bytes 6148
  7.2 5.4 %copy-start.2 = (bf16[512,256]{1,0:T(8,128)(2,1)S(1)}, bf16[512,256]{1,0:T(8,128)(2,1)}, u32[]{:S(2)}) copy-start(bf16[512,256]{1,0:T(8,128)(2,1)} %param.9) | copy-start | bytes 786436
  7.2 6.5 %copy-start.1 = (bf16[64,6480]{1,0:T(8,128)(2,1)S(1)}, bf16[64,6480]{1,0:T(8,128)(2,1)}, u32[]{:S(2)}) copy-start(bf16[64,6480]{1,0:T(8,128)(2,1)} %param.6) | copy-start | bytes 2488324
  7.2 82.9 %all-gather.3.cloned.1.call-start = ((), (), s32[]{:S(2)}) async-start(), calls=%async_computation | async-start | bytes 1114112 | tf_op jit(solution)/shard_map/all_gather | solution.py:39
  13.6 5.3 %copy-start.6 = (u32[256]{0:T(256)S(1)}, u32[256]{0:T(256)}, u32[]{:S(2)}) copy-start(u32[256]{0:T(256)} %constant.32) | copy-start | bytes 3076
  13.6 5.9 %copy-start.5 = (u32[256]{0:T(256)S(1)}, u32[256]{0:T(256)}, u32[]{:S(2)}) copy-start(u32[256]{0:T(256)} %constant.27) | copy-start | bytes 3076
  13.6 91.5 %all-gather.5.cloned.1.call-start = ((), (), s32[]{:S(2)}) async-start(), calls=%async_computation.1 | async-start | bytes 1114112 | tf_op jit(solution)/shard_map/all_gather | solution.py:43
  442.1 43.8 %copy-start.3 = (f32[1024]{0:T(1024)}, f32[1024]{0:T(1024)S(1)}, u32[]{:S(2)}) copy-start(f32[1024]{0:T(1024)S(1)} %add_multiply_fusion.1) | copy-start | bytes 12292
Sparse Core Ops, SparseCore 0:
  13.7 49.8 all-gather.2
  65.4 39.5 all-gather.4
where the time goes:
time: 518 us; the launch traced here: 517 us
  blocking collectives  431 us (83%)
  other arithmetic  33.6 us (6%)
  matrix products  18.2 us (4%)
  between operations  15.5 us (3%)
  waiting for transfers between devices  15 us (3%)
    pmax x3, blocking collectives, reduce_rows(): largest = lax.pmax(jnp.max(scaled, axis=0), 'row')  113 us
    pmax x3, blocking collectives, reduce_cols(): largest = lax.pmax(jnp.max(scaled, axis=1), 'col')  93.9 us
    psum x3, blocking collectives, reduce_cols(): lax.psum(jnp.sum(jnp.exp(scaled - largest[:, None]), axis=1), 'col')  85.5 us
    psum x3, blocking collectives, reduce_rows(): lax.psum(jnp.sum(jnp.exp(scaled - largest[None, :]), axis=0), 'row')  70.7 us
    unnamed x2, blocking collectives  68.3 us
    all_gather x1, waiting for transfers between devices, body(): lax.all_gather(ref_feat, 'row', axis=0, tiled=True)  14.9 us
  transfers between devices with their start and end apart: 2, of which 1 were waited for; matrix products, arithmetic and copies ran while one was open for 1% of the time, Pallas kernels for 0%

commit v1 on v0

--- a/solution.py
+++ b/solution.py
@@ -24,7 +24,9 @@
 
 def reduce_rows(scaled):
     largest = lax.pmax(jnp.max(scaled, axis=0), "row")
-    totals = lax.psum(jnp.sum(jnp.exp(scaled - largest[None, :]), axis=0), "row")
+    totals = jnp.sum(
+        lax.all_gather(jnp.sum(jnp.exp(scaled - largest[None, :]), axis=0), "row"), axis=0
+    )
     return -EPSILON * (largest + jnp.log(totals))
 
 

time: 518 us -> 491 us (0.948)
  blocking collectives: 431 us -> 404 us
    psum x3 -> x0, blocking collectives: 70.7 us -> none  [reduce_rows(): lax.psum(jnp.sum(jnp.exp(scaled - largest[None, :]), axis=0), 'row')]
    all_gather x0 -> x3, blocking collectives: none -> 44.4 us  [reduce_rows(): lax.all_gather(jnp.sum(jnp.exp(scaled - largest[None, :]), axis=0), 'row')]
where the time goes in v1:
time: 491 us; the launch traced here: 490 us
  blocking collectives  404 us (82%)
  other arithmetic  33.6 us (7%)
  matrix products  18.2 us (4%)
  between operations  15.6 us (3%)
  waiting for transfers between devices  15 us (3%)
    pmax x3, blocking collectives, reduce_rows(): largest = lax.pmax(jnp.max(scaled, axis=0), 'row')  112 us
    pmax x3, blocking collectives, reduce_cols(): largest = lax.pmax(jnp.max(scaled, axis=1), 'col')  93.9 us
    psum x3, blocking collectives, reduce_cols(): lax.psum(jnp.sum(jnp.exp(scaled - largest[:, None]), axis=1), 'col')  85.6 us
    unnamed x2, blocking collectives  68.3 us
    all_gather x3, blocking collectives, reduce_rows(): lax.all_gather(jnp.sum(jnp.exp(scaled - largest[None, :]), axis=0), 'row')  44.4 us
    all_gather x1, waiting for transfers between devices, body(): lax.all_gather(ref_feat, 'row', axis=0, tiled=True)  14.9 us
    reduce_sum x3, other arithmetic, reduce_cols(): jnp.sum(jnp.exp(scaled - largest[:, None]), axis=1)  9.88 us
  transfers between devices with their start and end apart: 2, of which 1 were waited for; matrix products, arithmetic and copies ran while one was open for 1% of the time, Pallas kernels for 0%

profile of v1, /device:TPU:1, one launch (start us, length us, event | category | flops | bytes accessed | tf_op | source)
XLA Modules:
  0.0 489.9 jit_solution(3651629564114793598)
XLA Ops:
  7.3 1.1 copy-done
  8.4 4.1 fusion.7
  12.6 1.0 multiply_reduce_fusion.1
  13.7 4.1 fusion.6
  17.8 1.0 multiply_reduce_fusion
  21.8 34.3 %all-reduce = f32[1024]{0:T(1024)S(1)} all-reduce(f32[1024]{0:T(1024)S(1)} %dynamic-update-slice), channel_id=1, replica_groups=mesh['row'=16,'col'=16] {'col'}, use_global_device_ids=true, to_apply=%add | all-reduce | flops 1024 | bytes 8192
  56.1 34.0 %all-reduce.1 = f32[1024]{0:T(1024)S(1)} all-reduce(f32[1024]{0:T(1024)S(1)} %dynamic-update-slice.1), channel_id=1, replica_groups=mesh['row'=16,'col'=16] {'row'}, use_global_device_ids=true, to_apply=%add.1 | all-reduce | flops 1024 | bytes 8192
  90.2 14.9 %all-gather.8.cloned.1.call-done = f32[1024,256]{1,0:T(8,128)} async-done(((f32[64,256]{1,0:T(8,128)}), f32[1024,256]{1,0:T(8,128)}) %all-gather.8.cloned.1.call-update) | async-done | bytes 1048592 | tf_op jit(solution)/shard_map/all_gather | solution.py:45
  105.1 7.9 %fusion = (f32[1024]{0:T(1024)S(1)}, f32[1024,1024]{1,0:T(8,128)}) fusion(f32[1024,256]{1,0:T(8,128)} %all-gather.6.cloned.1.call-done, f32[1024,256]{1,0:T(8,128)} %all-gather.8.cloned.1.call-done, f32[1024]{0:T(1024)S(1)} %all-reduce.1, f32[1024]{0:T(1024)S(1)} %all-reduce), kind=kOutput, calls=%fused_computation.13 | convolution fusion | flops 3229613056 | bytes 6303744 | tf_op jit(solution)/shard_map/dot_general | solution.py:52
  113.0 33.2 %pmax.42 = f32[1024]{0:T(1024)S(1)} all-reduce(f32[1024]{0:T(1024)S(1)} %get-tuple-element.6), channel_id=1, replica_groups=mesh['row'=16,'col'=16] {'col'}, use_global_device_ids=true, to_apply=%region_3.0 | all-reduce | flops 1024 | bytes 8192 | tf_op jit(solution)/shard_map/pmax | solution.py:20
  146.2 3.3 exponential_reduce_fusion.5
  149.5 28.5 %psum.21 = f32[1024]{0:T(1024)S(1)} all-reduce(f32[1024]{0:T(1024)S(1)} %exponential_reduce_fusion.5), channel_id=1, replica_groups=mesh['row'=16,'col'=16] {'col'}, use_global_device_ids=true, to_apply=%region_5.0 | all-reduce | flops 1024 | bytes 8192 | tf_op jit(solution)/shard_map/psum | solution.py:21
  178.0 2.8 fusion.1
  180.8 37.2 %pmax.43 = f32[1024]{0:T(1024)S(1)} all-reduce(f32[1024]{0:T(1024)S(1)} %fusion.1), channel_id=1, replica_groups=mesh['row'=16,'col'=16] {'row'}, use_global_device_ids=true, to_apply=%region_7.0 | all-reduce | flops 1024 | bytes 8192 | tf_op jit(solution)/shard_map/pmax | solution.py:26
  218.1 3.2 exponential_reduce_fusion.4
  221.3 14.8 %all-gather = f32[16384]{0:T(1024)S(1)} all-gather(f32[1024]{0:T(1024)S(1)} %exponential_reduce_fusion.4), channel_id=2, replica_groups=mesh['row'=16,'col'=16] {'row'}, dimensions={0}, use_global_device_ids=true | all-gather | bytes 69632 | tf_op jit(solution)/shard_map/all_gather | solution.py:28
  236.2 2.8 fusion.2
  239.0 30.4 %pmax.44 = f32[1024]{0:T(1024)S(1)} all-reduce(f32[1024]{0:T(1024)S(1)} %fusion.2), channel_id=1, replica_groups=mesh['row'=16,'col'=16] {'col'}, use_global_device_ids=true, to_apply=%region_11.0 | all-reduce | flops 1024 | bytes 8192 | tf_op jit(solution)/shard_map/pmax | solution.py:20
  269.4 3.3 exponential_reduce_fusion.3
  272.7 28.5 %psum.22 = f32[1024]{0:T(1024)S(1)} all-reduce(f32[1024]{0:T(1024)S(1)} %exponential_reduce_fusion.3), channel_id=1, replica_groups=mesh['row'=16,'col'=16] {'col'}, use_global_device_ids=true, to_apply=%region_13.0 | all-reduce | flops 1024 | bytes 8192 | tf_op jit(solution)/shard_map/psum | solution.py:21
  301.2 2.8 fusion.3
  304.0 37.3 %pmax.45 = f32[1024]{0:T(1024)S(1)} all-reduce(f32[1024]{0:T(1024)S(1)} %fusion.3), channel_id=1, replica_groups=mesh['row'=16,'col'=16] {'row'}, use_global_device_ids=true, to_apply=%region_15.0 | all-reduce | flops 1024 | bytes 8192 | tf_op jit(solution)/shard_map/pmax | solution.py:26
  341.3 3.2 exponential_reduce_fusion.2
  344.5 14.8 %all-gather.1 = f32[16384]{0:T(1024)S(1)} all-gather(f32[1024]{0:T(1024)S(1)} %exponential_reduce_fusion.2), channel_id=3, replica_groups=mesh['row'=16,'col'=16] {'row'}, dimensions={0}, use_global_device_ids=true | all-gather | bytes 69632 | tf_op jit(solution)/shard_map/all_gather | solution.py:28
  359.4 2.8 fusion.4
  362.2 30.2 %pmax.46 = f32[1024]{0:T(1024)S(1)} all-reduce(f32[1024]{0:T(1024)S(1)} %fusion.4), channel_id=1, replica_groups=mesh['row'=16,'col'=16] {'col'}, use_global_device_ids=true, to_apply=%region_19.0 | all-reduce | flops 1024 | bytes 8192 | tf_op jit(solution)/shard_map/pmax | solution.py:20
  392.4 3.3 exponential_reduce_fusion.1
  395.7 28.5 %psum.23 = f32[1024]{0:T(1024)S(1)} all-reduce(f32[1024]{0:T(1024)S(1)} %exponential_reduce_fusion.1), channel_id=1, replica_groups=mesh['row'=16,'col'=16] {'col'}, use_global_device_ids=true, to_apply=%region_21.0 | all-reduce | flops 1024 | bytes 8192 | tf_op jit(solution)/shard_map/psum | solution.py:21
  424.2 2.8 fusion.5
  427.1 37.2 %pmax.47 = f32[1024]{0:T(1024)S(1)} all-reduce(f32[1024]{0:T(1024)S(1)} %fusion.5), channel_id=1, replica_groups=mesh['row'=16,'col'=16] {'row'}, use_global_device_ids=true, to_apply=%region_23.0 | all-reduce | flops 1024 | bytes 8192 | tf_op jit(solution)/shard_map/pmax | solution.py:26
  464.3 3.2 exponential_reduce_fusion
  467.5 14.8 %all-gather.2 = f32[16384]{0:T(1024)S(1)} all-gather(f32[1024]{0:T(1024)S(1)} %exponential_reduce_fusion), channel_id=4, replica_groups=mesh['row'=16,'col'=16] {'row'}, dimensions={0}, use_global_device_ids=true | all-gather | bytes 69632 | tf_op jit(solution)/shard_map/all_gather | solution.py:28
  (37 shorter events, 2.6 us)
Async XLA Ops:
  7.2 1.2 copy-start
  7.2 6.5 %copy-start.4 = (f32[512]{0:T(512)S(1)}, f32[512]{0:T(512)}, u32[]{:S(2)}) copy-start(f32[512]{0:T(512)} %param.8) | copy-start | bytes 6148
  7.2 5.4 %copy-start.2 = (bf16[512,256]{1,0:T(8,128)(2,1)S(1)}, bf16[512,256]{1,0:T(8,128)(2,1)}, u32[]{:S(2)}) copy-start(bf16[512,256]{1,0:T(8,128)(2,1)} %param.9) | copy-start | bytes 786436
  7.2 6.5 %copy-start.1 = (bf16[64,6480]{1,0:T(8,128)(2,1)S(1)}, bf16[64,6480]{1,0:T(8,128)(2,1)}, u32[]{:S(2)}) copy-start(bf16[64,6480]{1,0:T(8,128)(2,1)} %param.6) | copy-start | bytes 2488324
  7.2 82.9 %all-gather.6.cloned.1.call-start = ((), (), s32[]{:S(2)}) async-start(), calls=%async_computation | async-start | bytes 1114112 | tf_op jit(solution)/shard_map/all_gather | solution.py:41
  13.6 5.3 %copy-start.6 = (u32[256]{0:T(256)S(1)}, u32[256]{0:T(256)}, u32[]{:S(2)}) copy-start(u32[256]{0:T(256)} %constant.27) | copy-start | bytes 3076
  13.6 5.9 %copy-start.5 = (u32[256]{0:T(256)S(1)}, u32[256]{0:T(256)}, u32[]{:S(2)}) copy-start(u32[256]{0:T(256)} %constant.32) | copy-start | bytes 3076
  13.6 91.5 %all-gather.8.cloned.1.call-start = ((), (), s32[]{:S(2)}) async-start(), calls=%async_computation.1 | async-start | bytes 1114112 | tf_op jit(solution)/shard_map/all_gather | solution.py:45
  424.2 43.3 %copy-start.3 = (f32[1024]{0:T(1024)}, f32[1024]{0:T(1024)S(1)}, u32[]{:S(2)}) copy-start(f32[1024]{0:T(1024)S(1)} %add_multiply_fusion.1) | copy-start | bytes 12292
Sparse Core Ops, SparseCore 0:
  13.7 49.8 all-gather.5
  65.4 39.5 all-gather.7
